TPU v7x, 32 devices: a whole 2x2x4 slice. The times are simulated.
32 devices in a mesh: ctx: 8 (over z, y), exp: 4 (over x, core).
Axes of the slice: x: 2, y: 2, z: 4, core: 2. Of those that a mesh axis runs over, the one named last changes fastest.
Arguments:
- residual: bfloat16 [1024, 6144], P('ctx', 'exp'), may hold values from -6 to 6
- query_rows: bfloat16 [1024, 6144], P('ctx', 'exp'), may hold values from -2 to 2
- key_rows: bfloat16 [1024, 6144], P('ctx', 'exp'), may hold values from -2 to 2
- value_rows: bfloat16 [1024, 6144], P('ctx', 'exp'), may hold values from -6 to 6
- log_decay: float32 [1024, 48], P('ctx', 'exp'), may hold values from -1 to 0
- norm_gain: bfloat16 [6144], P('exp'), may hold values from 0.5 to 1.5
- expert_ids: int32 [1024, 2], P('ctx'), may hold values from 0 to 3, all different within a row; in each aligned block of 128 rows (0 to 127, 128 to 255, ...) at most 96 rows name the same one
- gate_weights: float32 [1024, 2], P('ctx'), may hold values from 0.2 to 1
- w_gate: bfloat16 [4, 6144, 9216], P('exp', None, 'ctx'), may hold values from -0.078125 to 0.078125
- w_up: bfloat16 [4, 6144, 9216], P('exp', None, 'ctx'), may hold values from -0.078125 to 0.078125
- w_down: bfloat16 [4, 9216, 6144], P('exp', 'ctx'), may hold values from -0.0625 to 0.0625
Outputs:
- mixed: bfloat16 [1024, 6144], P('ctx', 'exp')
Inputs may be any that keep to these rules, and one draw needn't show every extreme that they name: `expert_ids`: each token names two different experts; among the 128 tokens of one block at most 96 name any one expert, and in every draw some expert is named by exactly 96 tokens of some block.
All inputs are finite; a program needn't handle non-finite values.
Results may differ from a plain program's by a relative error of at most 0.015.
Values may be sent and summed in bfloat16 or wider, within the bound.
No kernel may reach another device: no remote copies, remote signals or barrier semaphores. Data moves between devices by JAX's collectives and lax.ppermute only.
A program may use at most 128 MiB of HBM per device.

v0:
```python
import jax
import jax.numpy as jnp
from jax import lax
from jax.sharding import PartitionSpec as P

HEAD = 128
precise = lax.Precision.HIGHEST


def from_behind(value, axis, steps):
    count = lax.axis_size(axis)
    initial, last = (max(0, -steps), min(count, count - steps))
    return lax.ppermute(value, axis, [(source, source + steps) for source in range(initial, last)])


def matmul(left, right):
    return jnp.dot(left, right, preferred_element_type=jnp.float32)


def span_parts(query_blk, key_blk, value_blk, decay_blk):
    cumul = jnp.cumsum(decay_blk, axis=0)
    length = decay_blk.shape[0]
    causal = (jnp.arange(length)[:, None] >= jnp.arange(length)[None, :])[:, :, None]
    spread = cumul[:, None, :] - cumul[None, :, :]
    fading = jnp.where(causal, jnp.exp(jnp.where(causal, spread, 0.0)), 0.0)
    query_f = query_blk.astype(jnp.float32)
    key_f = key_blk.astype(jnp.float32)
    value_f = value_blk.astype(jnp.float32)
    scores = jnp.einsum("thd,uhd->htu", query_f, key_f) * jnp.transpose(fading, (2, 0, 1))
    scores = lax.optimization_barrier(scores.astype(jnp.bfloat16))
    inside = jnp.einsum("htu,uhd->thd", scores.astype(jnp.float32), value_f)
    tail = jnp.exp(cumul[-1][None, :] - cumul)
    local = jnp.einsum("uhd,uhe->hde", key_f * tail[:, :, None], value_f, precision=precise)
    return (inside, cumul, query_f, jnp.exp(cumul[-1]), local)


def head_norm(attended, gain):
    meansq = jnp.mean(attended * attended, axis=-1, keepdims=True)
    return attended * lax.rsqrt(meansq + 1e-05) * gain


def per_device(
    residual,
    query_rows,
    key_rows,
    value_rows,
    log_decay,
    norm_gain,
    expert_ids,
    gate_weights,
    w_gate,
    w_up,
    w_down,
):
    token_count, columns = residual.shape
    heads = columns // HEAD
    experts = lax.axis_size("exp")
    capacity = 3 * token_count // experts
    shaped = (token_count, heads, HEAD)
    inside, cumul, query_f, factor, local = span_parts(
        query_rows.reshape(shaped), key_rows.reshape(shaped), value_rows.reshape(shaped), log_decay
    )

    def relay_step(index, incoming):
        total = factor[:, None, None] * incoming + local
        return from_behind(total.astype(jnp.bfloat16), "ctx", 1).astype(total.dtype)

    incoming = lax.fori_loop(0, lax.axis_size("ctx") - 1, relay_step, jnp.zeros_like(local))
    carried = jnp.exp(cumul)[:, :, None] * jnp.einsum(
        "thd,hde->the", query_f, incoming, precision=precise
    )
    attended = inside + carried
    normed = head_norm(attended, norm_gain.astype(jnp.float32).reshape(heads, HEAD)).reshape(
        token_count, columns
    )
    hidden = (residual.astype(jnp.float32) + normed).astype(jnp.bfloat16)
    flat_ids = expert_ids.reshape(2 * token_count)
    onehot = (flat_ids[:, None] == jnp.arange(experts, dtype=jnp.int32)[None, :]).astype(jnp.int32)
    earlier_count = jnp.cumsum(onehot, axis=0) - onehot
    slots = jnp.sum(earlier_count * onehot, axis=1)
    places = flat_ids * capacity + slots
    select = (jnp.arange(experts * capacity, dtype=jnp.int32)[:, None] == places[None, :]).astype(
        jnp.float32
    )
    select = select.reshape(experts * capacity, token_count, 2).sum(axis=2).astype(jnp.bfloat16)
    buckets = matmul(select, hidden).astype(jnp.bfloat16).reshape(experts, capacity, columns)
    arrived = lax.all_to_all(buckets, "exp", split_axis=0, concat_axis=2, tiled=True).reshape(
        capacity, experts * columns
    )
    gate_local = w_gate[0]
    up_local = w_up[0]
    down_local = w_down[0]
    piece = lax.all_gather(arrived, "ctx", axis=0, tiled=True)
    activations = (jax.nn.silu(matmul(piece, gate_local)) * matmul(piece, up_local)).astype(
        jnp.bfloat16
    )
    summed = lax.psum_scatter(
        matmul(activations, down_local).astype(jnp.bfloat16), "ctx", scatter_dimension=0, tiled=True
    )
    expert_out = summed.reshape(1, capacity, experts * columns)
    returned = lax.all_to_all(expert_out, "exp", split_axis=2, concat_axis=0, tiled=True).reshape(
        experts * capacity, columns
    )
    picked = jnp.take(returned, places, axis=0).astype(jnp.float32).reshape(token_count, 2, columns)
    mixed = hidden.astype(jnp.float32) + jnp.sum(gate_weights[:, :, None] * picked, axis=1)
    return mixed.astype(jnp.bfloat16)


def solution(mesh):
    return jax.shard_map(
        per_device,
        mesh=mesh,
        in_specs=(
            P("ctx", "exp"),
            P("ctx", "exp"),
            P("ctx", "exp"),
            P("ctx", "exp"),
            P("ctx", "exp"),
            P("exp"),
            P("ctx", None),
            P("ctx", None),
            P("exp", None, "ctx"),
            P("exp", None, "ctx"),
            P("exp", "ctx", None),
        ),
        out_specs=P("ctx", "exp"),
        check_vma=False,
    )
```

profile of v0, /device:TPU:0, one launch (start us, length us, event | category | flops | bytes accessed | tf_op | source)
XLA Modules:
  0.0 559.8 jit_solution(8698001081078087218)
XLA Ops:
  14.6 81.0 %while.11 = (s32[]{:T(128)}, f32[12,128,128]{2,1,0:T(8,128)S(1)}, f32[12]{0:T(128)S(1)}, f32[12,128,128]{2,1,0:T(8,128)S(1)}, s32[]{:T(128)}, /*index=5*/s32[]{:T(128)}) while((s32[]{:T(128)}, f32[12,128,128]{2,1,0:T(8,128)S(1)}, f32[12]{0:T(128)S(1)}, f32[12,128,128]{2,1,0:T(8,128)S(1)}, s32[]{:T(128)}, /*index=5*/s32[]{:T(128)}) %tuple.25), condition=%wide.region_2.3_spmd.clone, body=%wide.region_1.2_spmd.clone.sunk | while | flops 983043 | bytes 4718759 | solution.py:68
  14.7 4.9 collective-permute-start
  19.7 8.3 %collective-permute-done = bf16[12,128,128]{2,1,0:T(8,128)(2,1)S(1)} collective-permute-done((bf16[12,128,128]{2,1,0:T(8,128)(2,1)S(1)}, bf16[12,128,128]{2,1,0:T(8,128)(2,1)S(1)}, u32[]{:S(2)}, u32[]{:S(2)}) %collective-permute-start) | collective-permute-done | bytes 393248 | tf_op jit(solution)/shard_map/while/body/eval_jaxpr/ppermute | solution.py:13
  32.7 7.5 %collective-permute-done = bf16[12,128,128]{2,1,0:T(8,128)(2,1)S(1)} collective-permute-done((bf16[12,128,128]{2,1,0:T(8,128)(2,1)S(1)}, bf16[12,128,128]{2,1,0:T(8,128)(2,1)S(1)}, u32[]{:S(2)}, u32[]{:S(2)}) %collective-permute-start) | collective-permute-done | bytes 393248 | tf_op jit(solution)/shard_map/while/body/eval_jaxpr/ppermute | solution.py:13
  44.8 6.6 %collective-permute-done = bf16[12,128,128]{2,1,0:T(8,128)(2,1)S(1)} collective-permute-done((bf16[12,128,128]{2,1,0:T(8,128)(2,1)S(1)}, bf16[12,128,128]{2,1,0:T(8,128)(2,1)S(1)}, u32[]{:S(2)}, u32[]{:S(2)}) %collective-permute-start) | collective-permute-done | bytes 393248 | tf_op jit(solution)/shard_map/while/body/eval_jaxpr/ppermute | solution.py:13
  51.7 5.3 collective-permute-start
  57.0 5.8 %collective-permute-done = bf16[12,128,128]{2,1,0:T(8,128)(2,1)S(1)} collective-permute-done((bf16[12,128,128]{2,1,0:T(8,128)(2,1)S(1)}, bf16[12,128,128]{2,1,0:T(8,128)(2,1)S(1)}, u32[]{:S(2)}, u32[]{:S(2)}) %collective-permute-start) | collective-permute-done | bytes 393248 | tf_op jit(solution)/shard_map/while/body/eval_jaxpr/ppermute | solution.py:13
  63.0 5.3 collective-permute-start
  68.3 5.3 collective-permute-done
  73.8 5.3 collective-permute-start
  79.1 5.3 collective-permute-done
  84.6 5.5 collective-permute-start
  90.2 5.3 collective-permute-done
  99.9 18.4 %all_to_all.30 = bf16[4,96,1536]{2,1,0:T(8,128)(2,1)S(1)} all-to-all(bf16[4,96,1536]{2,1,0:T(8,128)(2,1)S(1)} %bitcast.83), channel_id=1, replica_groups=mesh['ctx'=8,'exp'=4] {'exp'}, dimensions={0} | all-to-all | bytes 2359296 | tf_op jit(solution)/shard_map/all_to_all | solution.py:87
  120.7 140.3 %all-gather.2.cloned.1.call-done = bf16[768,6144]{1,0:T(8,128)(2,1)} async-done(((bf16[96,6144]{1,0:T(8,128)(2,1)}), bf16[768,6144]{1,0:T(8,128)(2,1)}) %all-gather.2.cloned.1.call-update) | async-done | bytes 9437200 | tf_op jit(solution)/shard_map/all_gather | solution.py:93
  260.9 16.2 %fusion.6 = f32[768,1152]{1,0:T(8,128)S(1)} fusion(bf16[768,6144]{1,0:T(8,128)(2,1)} %all-gather.2.cloned.1.call-done, bf16[1,6144,1152]{2,1,0:T(8,128)(2,1)} %param.21), kind=kOutput, calls=%fused_computation.8 | convolution fusion | flops 10871635968 | bytes 27131904 | tf_op jit(solution)/shard_map/dot_general | solution.py:17
  277.1 17.1 %fusion.14 = bf16[768,1152]{1,0:T(8,128)(2,1)S(1)} fusion(bf16[768,6144]{1,0:T(8,128)(2,1)} %all-gather.2.cloned.1.call-done, bf16[1,6144,1152]{2,1,0:T(8,128)(2,1)} %param.22, f32[768,1152]{1,0:T(8,128)S(1)} %fusion.6), kind=kOutput, calls=%fused_computation.12 | convolution fusion | flops 10876944384 | bytes 28901376 | tf_op jit(solution)/shard_map/dot_general | solution.py:17
  294.2 14.6 %fusion.8 = bf16[768,6144]{1,0:T(8,128)(2,1)} fusion(bf16[768,1152]{1,0:T(8,128)(2,1)S(1)} %fusion.14, bf16[1,1152,6144]{2,1,0:T(8,128)(2,1)S(1)} %bitcast.100), kind=kOutput, calls=%fused_computation.10 | convolution fusion | flops 10876354560 | bytes 25362432 | tf_op jit(solution)/shard_map/dot_general | solution.py:17
  308.8 160.4 %reduce-scatter.2.cloned.1.call-done = bf16[96,6144]{1,0:T(8,128)(2,1)} async-done(((bf16[768,6144]{1,0:T(8,128)(2,1)}), bf16[96,6144]{1,0:T(8,128)(2,1)}) %reduce-scatter.2.cloned.1.call-update) | async-done | bytes 1179664 | tf_op jit(solution)/shard_map/reduce_scatter | solution.py:97
  469.3 6.7 %copy.139 = bf16[1,96,6144]{1,0,2:T(2,128)(2,1)S(1)} copy(bf16[1,96,6144]{2,1,0:T(8,128)(2,1)} %bitcast.94) | data formatting | bytes 2359296 | tf_op jit(solution)/shard_map/reshape | solution.py:100
  476.5 34.7 %reduce = bf16[6144,96]{1,0:T(8,128)(2,1)} reduce(bf16[6144,1,96]{2,1,0:T(2,128)(2,1)S(1)} %bitcast.80, bf16[]{:T(256)} %broadcast.110), dimensions={1}, to_apply=%bitcast.66.reduce_sub_computation | reduce | bytes 2359298
  511.2 4.8 reshape.169
  522.0 14.1 %all-to-all-done.1 = bf16[4,2,73728]{2,1,0:T(2,128)(2,1)} async-done(((bf16[4,2,73728]{2,1,0:T(2,128)(2,1)}), bf16[4,2,73728]{2,1,0:T(2,128)(2,1)}, u32[]{:S(2)}, u32[]{:S(2)}) %all-to-all-start.1) | async-done | bytes 1179680 | tf_op jit(solution)/shard_map/all_to_all | solution.py:101
  539.7 5.2 copy.140
  (105 shorter events, 43.1 us)
Async XLA Ops:
  6.5 254.4 %all-gather.2.cloned.1.call-start = ((), (), s32[]{:S(2)}) async-start(), calls=%async_computation.3 | async-start | bytes 10616832 | tf_op jit(solution)/shard_map/all_gather | solution.py:93
  14.7 13.3 %collective-permute-start = (bf16[12,128,128]{2,1,0:T(8,128)(2,1)S(1)}, bf16[12,128,128]{2,1,0:T(8,128)(2,1)S(1)}, u32[]{:S(2)}, u32[]{:S(2)}) collective-permute-start(bf16[12,128,128]{2,1,0:T(8,128)(2,1)S(1)} %fusion.44), channel_id=1, source_target_pairs={{0,4},{4,8},{8,12},{12,16},{16,20},{20,24},{24,28},{1,5},{5,9},{9,... | collective-permute-start | bytes 1179656 | tf_op jit(solution)/shard_map/while/body/eval_jaxpr/ppermute | solution.py:13
  28.3 11.9 %collective-permute-start = (bf16[12,128,128]{2,1,0:T(8,128)(2,1)S(1)}, bf16[12,128,128]{2,1,0:T(8,128)(2,1)S(1)}, u32[]{:S(2)}, u32[]{:S(2)}) collective-permute-start(bf16[12,128,128]{2,1,0:T(8,128)(2,1)S(1)} %fusion.44), channel_id=1, source_target_pairs={{0,4},{4,8},{8,12},{12,16},{16,20},{20,24},{24,28},{1,5},{5,9},{9,... | collective-permute-start | bytes 1179656 | tf_op jit(solution)/shard_map/while/body/eval_jaxpr/ppermute | solution.py:13
  40.4 11.0 %collective-permute-start = (bf16[12,128,128]{2,1,0:T(8,128)(2,1)S(1)}, bf16[12,128,128]{2,1,0:T(8,128)(2,1)S(1)}, u32[]{:S(2)}, u32[]{:S(2)}) collective-permute-start(bf16[12,128,128]{2,1,0:T(8,128)(2,1)S(1)} %fusion.44), channel_id=1, source_target_pairs={{0,4},{4,8},{8,12},{12,16},{16,20},{20,24},{24,28},{1,5},{5,9},{9,... | collective-permute-start | bytes 1179656 | tf_op jit(solution)/shard_map/while/body/eval_jaxpr/ppermute | solution.py:13
  51.7 11.0 %collective-permute-start = (bf16[12,128,128]{2,1,0:T(8,128)(2,1)S(1)}, bf16[12,128,128]{2,1,0:T(8,128)(2,1)S(1)}, u32[]{:S(2)}, u32[]{:S(2)}) collective-permute-start(bf16[12,128,128]{2,1,0:T(8,128)(2,1)S(1)} %fusion.44), channel_id=1, source_target_pairs={{0,4},{4,8},{8,12},{12,16},{16,20},{20,24},{24,28},{1,5},{5,9},{9,... | collective-permute-start | bytes 1179656 | tf_op jit(solution)/shard_map/while/body/eval_jaxpr/ppermute | solution.py:13
  63.0 10.6 %collective-permute-start = (bf16[12,128,128]{2,1,0:T(8,128)(2,1)S(1)}, bf16[12,128,128]{2,1,0:T(8,128)(2,1)S(1)}, u32[]{:S(2)}, u32[]{:S(2)}) collective-permute-start(bf16[12,128,128]{2,1,0:T(8,128)(2,1)S(1)} %fusion.44), channel_id=1, source_target_pairs={{0,4},{4,8},{8,12},{12,16},{16,20},{20,24},{24,28},{1,5},{5,9},{9,... | collective-permute-start | bytes 1179656 | tf_op jit(solution)/shard_map/while/body/eval_jaxpr/ppermute | solution.py:13
  73.8 10.6 %collective-permute-start = (bf16[12,128,128]{2,1,0:T(8,128)(2,1)S(1)}, bf16[12,128,128]{2,1,0:T(8,128)(2,1)S(1)}, u32[]{:S(2)}, u32[]{:S(2)}) collective-permute-start(bf16[12,128,128]{2,1,0:T(8,128)(2,1)S(1)} %fusion.44), channel_id=1, source_target_pairs={{0,4},{4,8},{8,12},{12,16},{16,20},{20,24},{24,28},{1,5},{5,9},{9,... | collective-permute-start | bytes 1179656 | tf_op jit(solution)/shard_map/while/body/eval_jaxpr/ppermute | solution.py:13
  84.6 10.8 %collective-permute-start = (bf16[12,128,128]{2,1,0:T(8,128)(2,1)S(1)}, bf16[12,128,128]{2,1,0:T(8,128)(2,1)S(1)}, u32[]{:S(2)}, u32[]{:S(2)}) collective-permute-start(bf16[12,128,128]{2,1,0:T(8,128)(2,1)S(1)} %fusion.44), channel_id=1, source_target_pairs={{0,4},{4,8},{8,12},{12,16},{16,20},{20,24},{24,28},{1,5},{5,9},{9,... | collective-permute-start | bytes 1179656 | tf_op jit(solution)/shard_map/while/body/eval_jaxpr/ppermute | solution.py:13
  95.5 1.3 copy-start.8
  95.5 3.5 copy-start.7
  95.6 3.7 copy-start.4
  95.6 3.8 copy-start.2
  97.4 21.8 %copy-start = (f32[128,1536]{1,0:T(8,128)}, f32[128,1536]{1,0:T(8,128)S(1)}, u32[]{:S(2)}) copy-start(f32[128,1536]{1,0:T(8,128)S(1)} %copy.130) | copy-start | bytes 2359300
  99.1 20.1 %copy-start.5 = (s32[256]{0:T(256)}, s32[256]{0:T(256)S(1)}, u32[]{:S(2)}) copy-start(s32[256]{0:T(256)S(1)} %fusion.27) | copy-start | bytes 3076
  120.4 348.8 %reduce-scatter.2.cloned.1.call-start = ((), (), s32[]{:S(2)}) async-start(), calls=%async_computation.4 | async-start | bytes 10616832 | tf_op jit(solution)/shard_map/reduce_scatter | solution.py:97
  260.9 33.3 %slice-start = ((s8[14155776]{0:T(1024)(128)(4,1)}), s8[4194304]{0:T(1024)(128)(4,1)S(1)}, s32[]{:S(2)}) async-start(s8[14155776]{0:T(1024)(128)(4,1)} %bitcast.99), calls=%async_computation.5 | async-start | bytes 8388608
  260.9 33.3 %slice-start.1 = ((s8[14155776]{0:T(1024)(128)(4,1)}), s8[4194304]{0:T(1024)(128)(4,1)S(1)}, s32[]{:S(2)}) async-start(s8[14155776]{0:T(1024)(128)(4,1)} %bitcast.99), calls=%async_computation.6 | async-start | bytes 8388608
  277.1 17.1 %slice-start.2 = ((s8[14155776]{0:T(1024)(128)(4,1)}), s8[4194304]{0:T(1024)(128)(4,1)S(1)}, s32[]{:S(2)}) async-start(s8[14155776]{0:T(1024)(128)(4,1)} %bitcast.99), calls=%async_computation.7 | async-start | bytes 8388608
  277.1 17.1 %slice-start.3 = ((s8[14155776]{0:T(1024)(128)(4,1)}), s8[1572864]{0:T(1024)(128)(4,1)S(1)}, s32[]{:S(2)}) async-start(s8[14155776]{0:T(1024)(128)(4,1)} %bitcast.99), calls=%async_computation.8 | async-start | bytes 3145728
  511.2 9.5 %copy-start.9 = (f32[128,2]{0,1:T(2,128)S(1)}, f32[128,2]{0,1:T(2,128)}, u32[]{:S(2)}) copy-start(f32[128,2]{0,1:T(2,128)} %param.20) | copy-start | bytes 3076
  511.2 10.2 %copy-start.6 = (s32[256]{0:T(256)S(1)}, s32[256]{0:T(256)}, u32[]{:S(2)}) copy-start(s32[256]{0:T(256)} %copy-done.5) | copy-start | bytes 3076
  516.0 20.2 %all-to-all-start.1 = ((bf16[4,2,73728]{2,1,0:T(2,128)(2,1)}), bf16[4,2,73728]{2,1,0:T(2,128)(2,1)}, u32[]{:S(2)}, u32[]{:S(2)}) async-start(bf16[4,2,73728]{2,1,0:T(2,128)(2,1)} %reshape.169), calls=%async_computation.2 | async-start | bytes 2359296 | tf_op jit(solution)/shard_map/all_to_all | solution.py:101
  547.0 1.9 copy-start.3
  547.0 5.0 copy-start.1
Sparse Core Ops, SparseCore 0:
  120.6 140.3 all-gather.1
  308.9 160.2 reduce-scatter.1
where the time goes:
time: 561 us; the launch traced here: 560 us
  waiting for transfers between devices  359 us (64%)
  matrix products  50.9 us (9%)
  other arithmetic  42.9 us (8%)
  starting transfers between devices  39.7 us (7%)
  local copies, waits for them, and re-layouts  35.1 us (6%)
  blocking collectives  18.4 us (3%)
  between operations  13.8 us (2%)
    reduce_scatter x1, waiting for transfers between devices, per_device(): lax.psum_scatter(matmul(activations, down_local).astype(jnp.bfloat16), 'c...  160 us
    all_gather x1, waiting for transfers between devices, per_device(): piece = lax.all_gather(arrived, 'ctx', axis=0, tiled=True)  140 us
    dot_general x4, matrix products, matmul(): return jnp.dot(left, right, preferred_element_type=jnp.float32)  48.2 us
    ppermute x7, waiting for transfers between devices, from_behind(): lax.ppermute(value, axis, [(source, source + steps) for source in range(i...  43.9 us
    ppermute x7, starting transfers between devices, from_behind(): lax.ppermute(value, axis, [(source, source + steps) for source in range(i...  35.2 us
    unnamed x4, other arithmetic  34.8 us
    all_to_all x1, blocking collectives, per_device(): lax.all_to_all(buckets, 'exp', split_axis=0, concat_axis=2, tiled=True)  18.4 us
    unnamed x38, local copies, waits for them, and re-layouts  16.1 us
  transfers between devices with their start and end apart: 10, of which 10 were waited for; matrix products, arithmetic and copies ran while one was open for 0% of the time, Pallas kernels for 0%

commit v1 on v0

--- a/solution.py
+++ b/solution.py
@@ -98,9 +98,19 @@
         matmul(activations, down_local).astype(jnp.bfloat16), "ctx", scatter_dimension=0, tiled=True
     )
     expert_out = summed.reshape(1, capacity, experts * columns)
-    returned = lax.all_to_all(expert_out, "exp", split_axis=2, concat_axis=0, tiled=True).reshape(
-        experts * capacity, columns
-    )
+
+    def _store_core(inner_x, mesh_ax):
+        return jnp.concatenate(
+            lax.all_to_all(
+                jnp.stack(jnp.split(inner_x, lax.axis_size(mesh_ax), 2), 0),
+                axis_name=mesh_ax,
+                split_axis=0,
+                concat_axis=0,
+            ),
+            0,
+        )
+
+    returned = _store_core(expert_out, "exp").reshape(experts * capacity, columns)
     picked = jnp.take(returned, places, axis=0).astype(jnp.float32).reshape(token_count, 2, columns)
     mixed = hidden.astype(jnp.float32) + jnp.sum(gate_weights[:, :, None] * picked, axis=1)
     return mixed.astype(jnp.bfloat16)

time: 561 us -> 504 us (0.90)
  other arithmetic: 42.9 us -> 8.75 us
  local copies, waits for them, and re-layouts: 35.1 us -> 12.6 us
    unnamed x4 -> x3, other arithmetic: 34.8 us -> 0.08 us
    unnamed x38 -> x25, local copies, waits for them, and re-layouts: 16.1 us -> 6.65 us
    all_to_all x3 -> x0, local copies, waits for them, and re-layouts: 7.32 us -> none  [per_device(): lax.all_to_all(expert_out, 'exp', split_axis=2, concat_axis=0, tiled=True)]
    reshape x1 -> x0, local copies, waits for them, and re-layouts: 6.75 us -> none  [per_device(): expert_out = summed.reshape(1, capacity, experts * columns)]
where the time goes in v1:
time: 504 us; the launch traced here: 503 us
  waiting for transfers between devices  360 us (71%)
  matrix products  50.8 us (10%)
  starting transfers between devices  39.1 us (8%)
  blocking collectives  18.4 us (4%)
  between operations  13.7 us (3%)
  local copies, waits for them, and re-layouts  12.6 us (2%)
  other arithmetic  8.75 us (2%)
    reduce_scatter x1, waiting for transfers between devices, per_device(): lax.psum_scatter(matmul(activations, down_local).astype(jnp.bfloat16), 'c...  160 us
    all_gather x1, waiting for transfers between devices, per_device(): piece = lax.all_gather(arrived, 'ctx', axis=0, tiled=True)  140 us
    dot_general x4, matrix products, matmul(): return jnp.dot(left, right, preferred_element_type=jnp.float32)  48.2 us
    ppermute x7, waiting for transfers between devices, from_behind(): lax.ppermute(value, axis, [(source, source + steps) for source in range(i...  43.9 us
    ppermute x7, starting transfers between devices, from_behind(): lax.ppermute(value, axis, [(source, source + steps) for source in range(i...  35.2 us
    all_to_all x1, blocking collectives, per_device(): lax.all_to_all(buckets, 'exp', split_axis=0, concat_axis=2, tiled=True)  18.4 us
    all_to_all x1, waiting for transfers between devices, _store_core(): lax.all_to_all(jnp.stack(jnp.split(inner_x, lax.axis_size(mesh_ax), 2), 0...  15 us
  transfers between devices with their start and end apart: 10, of which 10 were waited for; matrix products, arithmetic and copies ran while one was open for 0% of the time, Pallas kernels for 0%

profile of v1, /device:TPU:0, one launch (start us, length us, event | category | flops | bytes accessed | tf_op | source)
XLA Modules:
  0.0 503.3 jit_solution(3229506852879685229)
XLA Ops:
  14.5 80.9 %while.11 = (s32[]{:T(128)}, f32[12,128,128]{2,1,0:T(8,128)S(1)}, f32[12]{0:T(128)S(1)}, f32[12,128,128]{2,1,0:T(8,128)S(1)}, s32[]{:T(128)}, /*index=5*/s32[]{:T(128)}) while((s32[]{:T(128)}, f32[12,128,128]{2,1,0:T(8,128)S(1)}, f32[12]{0:T(128)S(1)}, f32[12,128,128]{2,1,0:T(8,128)S(1)}, s32[]{:T(128)}, /*index=5*/s32[]{:T(128)}) %tuple.28), condition=%wide.region_2.3_spmd.clone, body=%wide.region_1.2_spmd.clone.sunk | while | flops 983043 | bytes 4718759 | solution.py:68
  14.7 4.9 collective-permute-start
  19.6 8.3 %collective-permute-done = bf16[12,128,128]{2,1,0:T(8,128)(2,1)S(1)} collective-permute-done((bf16[12,128,128]{2,1,0:T(8,128)(2,1)S(1)}, bf16[12,128,128]{2,1,0:T(8,128)(2,1)S(1)}, u32[]{:S(2)}, u32[]{:S(2)}) %collective-permute-start) | collective-permute-done | bytes 393248 | tf_op jit(solution)/shard_map/while/body/eval_jaxpr/ppermute | solution.py:13
  28.2 4.4 collective-permute-start
  32.6 7.5 %collective-permute-done = bf16[12,128,128]{2,1,0:T(8,128)(2,1)S(1)} collective-permute-done((bf16[12,128,128]{2,1,0:T(8,128)(2,1)S(1)}, bf16[12,128,128]{2,1,0:T(8,128)(2,1)S(1)}, u32[]{:S(2)}, u32[]{:S(2)}) %collective-permute-start) | collective-permute-done | bytes 393248 | tf_op jit(solution)/shard_map/while/body/eval_jaxpr/ppermute | solution.py:13
  40.4 4.4 collective-permute-start
  44.8 6.6 %collective-permute-done = bf16[12,128,128]{2,1,0:T(8,128)(2,1)S(1)} collective-permute-done((bf16[12,128,128]{2,1,0:T(8,128)(2,1)S(1)}, bf16[12,128,128]{2,1,0:T(8,128)(2,1)S(1)}, u32[]{:S(2)}, u32[]{:S(2)}) %collective-permute-start) | collective-permute-done | bytes 393248 | tf_op jit(solution)/shard_map/while/body/eval_jaxpr/ppermute | solution.py:13
  51.7 5.2 %collective-permute-start = (bf16[12,128,128]{2,1,0:T(8,128)(2,1)S(1)}, bf16[12,128,128]{2,1,0:T(8,128)(2,1)S(1)}, u32[]{:S(2)}, u32[]{:S(2)}) collective-permute-start(bf16[12,128,128]{2,1,0:T(8,128)(2,1)S(1)} %fusion.44), channel_id=1, source_target_pairs={{0,4},{4,8},{8,12},{12,16},{16,20},{20,24},{24,28},{1,5},{5,9},{9,... | collective-permute-start | bytes 1179656 | tf_op jit(solution)/shard_map/while/body/eval_jaxpr/ppermute | solution.py:13
  56.9 5.8 %collective-permute-done = bf16[12,128,128]{2,1,0:T(8,128)(2,1)S(1)} collective-permute-done((bf16[12,128,128]{2,1,0:T(8,128)(2,1)S(1)}, bf16[12,128,128]{2,1,0:T(8,128)(2,1)S(1)}, u32[]{:S(2)}, u32[]{:S(2)}) %collective-permute-start) | collective-permute-done | bytes 393248 | tf_op jit(solution)/shard_map/while/body/eval_jaxpr/ppermute | solution.py:13
  62.9 5.3 %collective-permute-start = (bf16[12,128,128]{2,1,0:T(8,128)(2,1)S(1)}, bf16[12,128,128]{2,1,0:T(8,128)(2,1)S(1)}, u32[]{:S(2)}, u32[]{:S(2)}) collective-permute-start(bf16[12,128,128]{2,1,0:T(8,128)(2,1)S(1)} %fusion.44), channel_id=1, source_target_pairs={{0,4},{4,8},{8,12},{12,16},{16,20},{20,24},{24,28},{1,5},{5,9},{9,... | collective-permute-start | bytes 1179656 | tf_op jit(solution)/shard_map/while/body/eval_jaxpr/ppermute | solution.py:13
  68.2 5.3 %collective-permute-done = bf16[12,128,128]{2,1,0:T(8,128)(2,1)S(1)} collective-permute-done((bf16[12,128,128]{2,1,0:T(8,128)(2,1)S(1)}, bf16[12,128,128]{2,1,0:T(8,128)(2,1)S(1)}, u32[]{:S(2)}, u32[]{:S(2)}) %collective-permute-start) | collective-permute-done | bytes 393248 | tf_op jit(solution)/shard_map/while/body/eval_jaxpr/ppermute | solution.py:13
  73.7 5.3 %collective-permute-start = (bf16[12,128,128]{2,1,0:T(8,128)(2,1)S(1)}, bf16[12,128,128]{2,1,0:T(8,128)(2,1)S(1)}, u32[]{:S(2)}, u32[]{:S(2)}) collective-permute-start(bf16[12,128,128]{2,1,0:T(8,128)(2,1)S(1)} %fusion.44), channel_id=1, source_target_pairs={{0,4},{4,8},{8,12},{12,16},{16,20},{20,24},{24,28},{1,5},{5,9},{9,... | collective-permute-start | bytes 1179656 | tf_op jit(solution)/shard_map/while/body/eval_jaxpr/ppermute | solution.py:13
  79.1 5.3 %collective-permute-done = bf16[12,128,128]{2,1,0:T(8,128)(2,1)S(1)} collective-permute-done((bf16[12,128,128]{2,1,0:T(8,128)(2,1)S(1)}, bf16[12,128,128]{2,1,0:T(8,128)(2,1)S(1)}, u32[]{:S(2)}, u32[]{:S(2)}) %collective-permute-start) | collective-permute-done | bytes 393248 | tf_op jit(solution)/shard_map/while/body/eval_jaxpr/ppermute | solution.py:13
  84.6 5.6 %collective-permute-start = (bf16[12,128,128]{2,1,0:T(8,128)(2,1)S(1)}, bf16[12,128,128]{2,1,0:T(8,128)(2,1)S(1)}, u32[]{:S(2)}, u32[]{:S(2)}) collective-permute-start(bf16[12,128,128]{2,1,0:T(8,128)(2,1)S(1)} %fusion.44), channel_id=1, source_target_pairs={{0,4},{4,8},{8,12},{12,16},{16,20},{20,24},{24,28},{1,5},{5,9},{9,... | collective-permute-start | bytes 1179656 | tf_op jit(solution)/shard_map/while/body/eval_jaxpr/ppermute | solution.py:13
  90.1 5.3 %collective-permute-done = bf16[12,128,128]{2,1,0:T(8,128)(2,1)S(1)} collective-permute-done((bf16[12,128,128]{2,1,0:T(8,128)(2,1)S(1)}, bf16[12,128,128]{2,1,0:T(8,128)(2,1)S(1)}, u32[]{:S(2)}, u32[]{:S(2)}) %collective-permute-start) | collective-permute-done | bytes 393248 | tf_op jit(solution)/shard_map/while/body/eval_jaxpr/ppermute | solution.py:13
  99.8 18.4 %all_to_all.20 = bf16[4,96,1536]{2,1,0:T(8,128)(2,1)S(1)} all-to-all(bf16[4,96,1536]{2,1,0:T(8,128)(2,1)S(1)} %bitcast.86), channel_id=1, replica_groups=mesh['ctx'=8,'exp'=4] {'exp'}, dimensions={0} | all-to-all | bytes 2359296 | tf_op jit(solution)/shard_map/all_to_all | solution.py:87
  120.5 140.2 %all-gather.2.cloned.1.call-done = bf16[768,6144]{1,0:T(8,128)(2,1)} async-done(((bf16[96,6144]{1,0:T(8,128)(2,1)}), bf16[768,6144]{1,0:T(8,128)(2,1)}) %all-gather.2.cloned.1.call-update) | async-done | bytes 9437200 | tf_op jit(solution)/shard_map/all_gather | solution.py:93
  260.8 16.1 %fusion.6 = f32[768,1152]{1,0:T(8,128)S(1)} fusion(bf16[768,6144]{1,0:T(8,128)(2,1)} %all-gather.2.cloned.1.call-done, bf16[1,6144,1152]{2,1,0:T(8,128)(2,1)} %param.21), kind=kOutput, calls=%fused_computation.8 | convolution fusion | flops 10871635968 | bytes 27131904 | tf_op jit(solution)/shard_map/dot_general | solution.py:17
  277.0 17.1 %fusion.14 = bf16[768,1152]{1,0:T(8,128)(2,1)S(1)} fusion(bf16[768,6144]{1,0:T(8,128)(2,1)} %all-gather.2.cloned.1.call-done, bf16[1,6144,1152]{2,1,0:T(8,128)(2,1)} %param.22, f32[768,1152]{1,0:T(8,128)S(1)} %fusion.6), kind=kOutput, calls=%fused_computation.12 | convolution fusion | flops 10876944384 | bytes 28901376 | tf_op jit(solution)/shard_map/dot_general | solution.py:17
  294.1 14.5 %fusion.8 = bf16[768,6144]{1,0:T(8,128)(2,1)} fusion(bf16[768,1152]{1,0:T(8,128)(2,1)S(1)} %fusion.14, bf16[1,1152,6144]{2,1,0:T(8,128)(2,1)S(1)} %bitcast.102), kind=kOutput, calls=%fused_computation.10 | convolution fusion | flops 10876354560 | bytes 25362432 | tf_op jit(solution)/shard_map/dot_general | solution.py:17
  308.6 160.4 %reduce-scatter.2.cloned.1.call-done = bf16[96,6144]{1,0:T(8,128)(2,1)} async-done(((bf16[768,6144]{1,0:T(8,128)(2,1)}), bf16[96,6144]{1,0:T(8,128)(2,1)}) %reduce-scatter.2.cloned.1.call-update) | async-done | bytes 1179664 | tf_op jit(solution)/shard_map/reduce_scatter | solution.py:97
  471.5 3.7 all-to-all-start.1
  475.8 15.0 %all-to-all-done.1 = bf16[4,1,96,1536]{3,2,1,0:T(8,128)(2,1)S(1)} async-done(((bf16[4,1,96,1536]{3,2,1,0:T(8,128)(2,1)}), bf16[4,1,96,1536]{3,2,1,0:T(8,128)(2,1)S(1)}, u32[]{:S(2)}, u32[]{:S(2)}) %all-to-all-start.1) | async-done | bytes 1179680 | tf_op jit(solution)/shard_map/all_to_all | solution.py:104
  492.4 3.2 multiply_reduce_fusion
  (89 shorter events, 21.5 us)
Async XLA Ops:
  6.5 254.2 %all-gather.2.cloned.1.call-start = ((), (), s32[]{:S(2)}) async-start(), calls=%async_computation.3 | async-start | bytes 10616832 | tf_op jit(solution)/shard_map/all_gather | solution.py:93
  14.7 13.3 %collective-permute-start = (bf16[12,128,128]{2,1,0:T(8,128)(2,1)S(1)}, bf16[12,128,128]{2,1,0:T(8,128)(2,1)S(1)}, u32[]{:S(2)}, u32[]{:S(2)}) collective-permute-start(bf16[12,128,128]{2,1,0:T(8,128)(2,1)S(1)} %fusion.44), channel_id=1, source_target_pairs={{0,4},{4,8},{8,12},{12,16},{16,20},{20,24},{24,28},{1,5},{5,9},{9,... | collective-permute-start | bytes 1179656 | tf_op jit(solution)/shard_map/while/body/eval_jaxpr/ppermute | solution.py:13
  28.2 11.9 %collective-permute-start = (bf16[12,128,128]{2,1,0:T(8,128)(2,1)S(1)}, bf16[12,128,128]{2,1,0:T(8,128)(2,1)S(1)}, u32[]{:S(2)}, u32[]{:S(2)}) collective-permute-start(bf16[12,128,128]{2,1,0:T(8,128)(2,1)S(1)} %fusion.44), channel_id=1, source_target_pairs={{0,4},{4,8},{8,12},{12,16},{16,20},{20,24},{24,28},{1,5},{5,9},{9,... | collective-permute-start | bytes 1179656 | tf_op jit(solution)/shard_map/while/body/eval_jaxpr/ppermute | solution.py:13
  40.4 11.0 %collective-permute-start = (bf16[12,128,128]{2,1,0:T(8,128)(2,1)S(1)}, bf16[12,128,128]{2,1,0:T(8,128)(2,1)S(1)}, u32[]{:S(2)}, u32[]{:S(2)}) collective-permute-start(bf16[12,128,128]{2,1,0:T(8,128)(2,1)S(1)} %fusion.44), channel_id=1, source_target_pairs={{0,4},{4,8},{8,12},{12,16},{16,20},{20,24},{24,28},{1,5},{5,9},{9,... | collective-permute-start | bytes 1179656 | tf_op jit(solution)/shard_map/while/body/eval_jaxpr/ppermute | solution.py:13
  51.7 11.0 %collective-permute-start = (bf16[12,128,128]{2,1,0:T(8,128)(2,1)S(1)}, bf16[12,128,128]{2,1,0:T(8,128)(2,1)S(1)}, u32[]{:S(2)}, u32[]{:S(2)}) collective-permute-start(bf16[12,128,128]{2,1,0:T(8,128)(2,1)S(1)} %fusion.44), channel_id=1, source_target_pairs={{0,4},{4,8},{8,12},{12,16},{16,20},{20,24},{24,28},{1,5},{5,9},{9,... | collective-permute-start | bytes 1179656 | tf_op jit(solution)/shard_map/while/body/eval_jaxpr/ppermute | solution.py:13
  62.9 10.6 %collective-permute-start = (bf16[12,128,128]{2,1,0:T(8,128)(2,1)S(1)}, bf16[12,128,128]{2,1,0:T(8,128)(2,1)S(1)}, u32[]{:S(2)}, u32[]{:S(2)}) collective-permute-start(bf16[12,128,128]{2,1,0:T(8,128)(2,1)S(1)} %fusion.44), channel_id=1, source_target_pairs={{0,4},{4,8},{8,12},{12,16},{16,20},{20,24},{24,28},{1,5},{5,9},{9,... | collective-permute-start | bytes 1179656 | tf_op jit(solution)/shard_map/while/body/eval_jaxpr/ppermute | solution.py:13
  73.7 10.6 %collective-permute-start = (bf16[12,128,128]{2,1,0:T(8,128)(2,1)S(1)}, bf16[12,128,128]{2,1,0:T(8,128)(2,1)S(1)}, u32[]{:S(2)}, u32[]{:S(2)}) collective-permute-start(bf16[12,128,128]{2,1,0:T(8,128)(2,1)S(1)} %fusion.44), channel_id=1, source_target_pairs={{0,4},{4,8},{8,12},{12,16},{16,20},{20,24},{24,28},{1,5},{5,9},{9,... | collective-permute-start | bytes 1179656 | tf_op jit(solution)/shard_map/while/body/eval_jaxpr/ppermute | solution.py:13
  84.6 10.8 %collective-permute-start = (bf16[12,128,128]{2,1,0:T(8,128)(2,1)S(1)}, bf16[12,128,128]{2,1,0:T(8,128)(2,1)S(1)}, u32[]{:S(2)}, u32[]{:S(2)}) collective-permute-start(bf16[12,128,128]{2,1,0:T(8,128)(2,1)S(1)} %fusion.44), channel_id=1, source_target_pairs={{0,4},{4,8},{8,12},{12,16},{16,20},{20,24},{24,28},{1,5},{5,9},{9,... | collective-permute-start | bytes 1179656 | tf_op jit(solution)/shard_map/while/body/eval_jaxpr/ppermute | solution.py:13
  95.5 1.3 copy-start.3
  95.5 3.5 copy-start.2
  95.5 3.7 copy-start.1
  95.5 3.8 copy-start
  120.3 348.7 %reduce-scatter.2.cloned.1.call-start = ((), (), s32[]{:S(2)}) async-start(), calls=%async_computation.4 | async-start | bytes 10616832 | tf_op jit(solution)/shard_map/reduce_scatter | solution.py:97
  260.8 33.2 %slice-start = ((s8[14155776]{0:T(1024)(128)(4,1)}), s8[4194304]{0:T(1024)(128)(4,1)S(1)}, s32[]{:S(2)}) async-start(s8[14155776]{0:T(1024)(128)(4,1)} %bitcast.101), calls=%async_computation.5 | async-start | bytes 8388608
  260.8 33.3 %slice-start.1 = ((s8[14155776]{0:T(1024)(128)(4,1)}), s8[4194304]{0:T(1024)(128)(4,1)S(1)}, s32[]{:S(2)}) async-start(s8[14155776]{0:T(1024)(128)(4,1)} %bitcast.101), calls=%async_computation.6 | async-start | bytes 8388608
  276.9 17.1 %slice-start.2 = ((s8[14155776]{0:T(1024)(128)(4,1)}), s8[4194304]{0:T(1024)(128)(4,1)S(1)}, s32[]{:S(2)}) async-start(s8[14155776]{0:T(1024)(128)(4,1)} %bitcast.101), calls=%async_computation.7 | async-start | bytes 8388608
  276.9 17.1 %slice-start.3 = ((s8[14155776]{0:T(1024)(128)(4,1)}), s8[1572864]{0:T(1024)(128)(4,1)S(1)}, s32[]{:S(2)}) async-start(s8[14155776]{0:T(1024)(128)(4,1)} %bitcast.101), calls=%async_computation.8 | async-start | bytes 3145728
  469.0 6.7 %copy-start.4 = (f32[128,2]{0,1:T(2,128)S(1)}, f32[128,2]{0,1:T(2,128)}, u32[]{:S(2)}) copy-start(f32[128,2]{0,1:T(2,128)} %param.20) | copy-start | bytes 3076
  471.5 19.3 %all-to-all-start.1 = ((bf16[4,1,96,1536]{3,2,1,0:T(8,128)(2,1)}), bf16[4,1,96,1536]{3,2,1,0:T(8,128)(2,1)S(1)}, u32[]{:S(2)}, u32[]{:S(2)}) async-start(bf16[4,1,96,1536]{3,2,1,0:T(8,128)(2,1)} %pad_maximum_fusion), calls=%async_computation.2 | async-start | bytes 2359296 | tf_op jit(solution)/shard_map/all_to_all | solution.py:104
Sparse Core Ops, SparseCore 0:
  120.4 140.3 all-gather.1
  308.7 160.2 reduce-scatter.1
